TPU v7x, 32 devices: a whole 2x2x4 slice. The times are simulated.
32 devices in a mesh: tiles: 2 (over y), row: 8 (over z, x), col: 2 (over core).
Axes of the slice: x: 2, y: 2, z: 4, core: 2. Of those that a mesh axis runs over, the one named last changes fastest.
Arguments:
- layers: float32 [8, 4096, 4096], P('tiles', 'row', 'col'), parts along dimension 0, may hold values from -6 to 6
- unmixing: bfloat16 [4, 4, 4, 2048, 4096], P('tiles', None, None, ('row', 'col')), parts along dimension 0, may hold values from -2 to 2
Outputs:
- components: float32 [8, 4096, 4096], P('tiles', 'row', 'col'), parts along dimension 0
There are 2 independent parts, one for each index of `tiles`. A program takes and returns all parts, laid end to end along the dimension named above; each array names one. Nothing has to cross between parts.
All inputs are finite; a program needn't handle non-finite values.
Results may differ from a plain program's by a relative error of at most 0.0003.
Values sent between devices are 32-bit elements; how exact they have to be, the bound alone decides.
No kernel may reach another device: no remote copies, remote signals or barrier semaphores. Data moves between devices by JAX's collectives and lax.ppermute only.
A program may use at most 320 MiB of HBM per device.

v0:
```python
import math
import jax
import jax.numpy as jnp
from jax import lax
from jax.sharding import PartitionSpec as P


def phase_pair(first_len, second_len, period, sign):
    first = lax.broadcasted_iota(jnp.int32, (first_len, second_len), 0)
    second = lax.broadcasted_iota(jnp.int32, (first_len, second_len), 1)
    turns = (first * second % period).astype(jnp.float32)
    phase = turns * (sign * 2.0 * math.pi / period)
    return (jnp.cos(phase), jnp.sin(phase))


def contract_first(values, table):
    return jnp.einsum("...qp,qk->...pk", values, table, precision=lax.Precision.HIGHEST)


def contract_second(values, table):
    return jnp.einsum("...pk,pj->...jk", values, table, precision=lax.Precision.HIGHEST)


def fourier(real_in, imag_in, length, sign, in_len, out_len, real_only):
    inner_len = min(length, 128)
    outer_len = length // inner_len
    rows_in = in_len // outer_len
    rows_out = out_len // inner_len
    leading = real_in.shape[:-1]
    first_cos, first_sin = phase_pair(rows_in, inner_len, inner_len, sign)
    first_table = jnp.concatenate([first_cos, first_sin], axis=1)
    both = contract_first(real_in.reshape(leading + (rows_in, outer_len)), first_table)
    part_real = both[..., :inner_len]
    part_imag = both[..., inner_len:]
    if imag_in is not None:
        other = contract_first(imag_in.reshape(leading + (rows_in, outer_len)), first_table)
        part_real = part_real - other[..., inner_len:]
        part_imag = part_imag + other[..., :inner_len]
    twist_cos, twist_sin = phase_pair(outer_len, inner_len, length, sign)
    turned_real = part_real * twist_cos - part_imag * twist_sin
    turned_imag = part_real * twist_sin + part_imag * twist_cos
    stacked = jnp.concatenate([turned_real, turned_imag], axis=-2)
    second_cos, second_sin = phase_pair(outer_len, rows_out, outer_len, sign)
    table_real = jnp.concatenate([second_cos, -second_sin], axis=0)
    if real_only:
        result_real = contract_second(stacked, table_real)
        return result_real.reshape(leading + (out_len,))
    table_imag = jnp.concatenate([second_sin, second_cos], axis=0)
    combined = contract_second(stacked, jnp.concatenate([table_real, table_imag], axis=1))
    result_real = combined[..., :rows_out, :].reshape(leading + (out_len,))
    result_imag = combined[..., rows_out:, :].reshape(leading + (out_len,))
    return (result_real, result_imag)


def reorder_blocks(values, row_count, col_count):
    leading = values.shape[0]
    block = values.shape[1] // (row_count * col_count)
    width = values.shape[2]
    split = values.reshape(leading, col_count, row_count, block, width)
    return jnp.transpose(split, (0, 4, 2, 1, 3)).reshape(
        leading, width, row_count * col_count * block
    )


def shards(layers, unmixing):
    row_count = lax.axis_size("row")
    col_count = lax.axis_size("col")
    rows_len = layers.shape[1] * row_count
    cols_len = layers.shape[2] * col_count
    spec_real, spec_imag = fourier(
        lax.all_to_all(layers, "col", split_axis=1, concat_axis=2, tiled=True),
        None,
        cols_len,
        -1.0,
        cols_len,
        cols_len // 2,
        False,
    )
    moved_real, moved_imag = (
        lax.all_to_all(
            lax.all_to_all(spec_real, "row", split_axis=2, concat_axis=1, tiled=True),
            "col",
            split_axis=2,
            concat_axis=1,
            tiled=True,
        ),
        lax.all_to_all(
            lax.all_to_all(spec_imag, "row", split_axis=2, concat_axis=1, tiled=True),
            "col",
            split_axis=2,
            concat_axis=1,
            tiled=True,
        ),
    )
    line_real = reorder_blocks(moved_real, row_count, col_count)
    line_imag = reorder_blocks(moved_imag, row_count, col_count)
    wave_real, wave_imag = fourier(line_real, line_imag, rows_len, -1.0, rows_len, rows_len, False)
    mixed_real = None
    mixed_imag = None
    for layer_index in range(4):
        weight_real = unmixing[0, :, layer_index].astype(jnp.float32)
        weight_imag = unmixing[1, :, layer_index].astype(jnp.float32)
        layer_real = wave_real[layer_index][None]
        layer_imag = wave_imag[layer_index][None]
        term_real = weight_real * layer_real - weight_imag * layer_imag
        term_imag = weight_real * layer_imag + weight_imag * layer_real
        if mixed_real is None:
            mixed_real = term_real
            mixed_imag = term_imag
        else:
            mixed_real = mixed_real + term_real
            mixed_imag = mixed_imag + term_imag
    back_real, back_imag = fourier(mixed_real, mixed_imag, rows_len, 1.0, rows_len, rows_len, False)
    scale = 2.0 / (rows_len * cols_len)
    sent_real, sent_imag = (
        lax.all_to_all(
            lax.all_to_all(back_real, "row", split_axis=2, concat_axis=1, tiled=True),
            "col",
            split_axis=2,
            concat_axis=1,
            tiled=True,
        ),
        lax.all_to_all(
            lax.all_to_all(back_imag, "row", split_axis=2, concat_axis=1, tiled=True),
            "col",
            split_axis=2,
            concat_axis=1,
            tiled=True,
        ),
    )
    grid_real = reorder_blocks(sent_real, row_count, col_count)
    grid_imag = reorder_blocks(sent_imag, row_count, col_count)
    fields = fourier(grid_real, grid_imag, cols_len, 1.0, cols_len // 2, cols_len, True)
    fields = fields * scale
    return lax.all_to_all(fields, "col", split_axis=2, concat_axis=1, tiled=True)


def solution(mesh):
    in_specs = (P("tiles", "row", "col"), P("tiles", None, None, ("row", "col"), None))
    out_specs = P("tiles", "row", "col")
    return jax.shard_map(shards, mesh=mesh, in_specs=in_specs, out_specs=out_specs, check_vma=False)
```

profile of v0, /device:TPU:0, one launch (start us, length us, event | category | flops | bytes accessed | tf_op | source)
XLA Modules:
  0.0 1691.4 jit_solution(6777798758830967953)
XLA Ops:
  0.0 20.9 %copy.174 = f32[4,512,2048]{2,0,1:T(4,128)} copy(f32[4,512,2048]{2,1,0:T(8,128)} %param.2) | data formatting | bytes 33554432 | tf_op args[0]
  44.1 17.8 %copy.175 = f32[4,512,2048]{2,1,0:T(8,128)} copy(f32[4,512,2048]{2,0,1:T(4,128)} %all-to-all-done) | data formatting | bytes 33554432 | tf_op jit(solution)/shard_map/all_to_all | solution.py:71
  61.9 16.4 copy.176
  78.3 44.1 %fusion.8 = f32[4,256,32,256]{1,3,2,0:T(8,128)} fusion(f32[4,256,128,32]{1,3,2,0:T(8,128)} %bitcast.134, f32[128,128]{0,1:T(8,128)S(1)} %get-tuple-element.35, f32[128,128]{0,1:T(8,128)S(1)} %get-tuple-element.36), kind=kOutput, calls=%fused_computation.19 | convolution fusion | flops 12884934656 | bytes 50462720 | tf_op jit(solution)/shard_map/...qp,qk->...pk/dot_general | solution.py:17
  122.4 17.6 %multiply_subtract_fusion.1 = (f32[4,256,32,128]{1,3,2,0:T(8,128)S(1)}, f32[4,256,32,128]{1,3,2,0:T(8,128)}) fusion(f32[4,256,32,256]{1,3,2,0:T(8,128)} %fusion.8, f32[32,128]{1,0:T(8,128)S(1)} %get-tuple-element.37, f32[32,128]{1,0:T(8,128)S(1)} %get-tuple-element.38), kind=kLoop, calls=%fused_computation.18 | loop fusion | flops 25165824 | bytes 67141632 | tf_op jit(solution)/shard_map/sub | solution.py:40
  140.0 18.5 %pad_maximum_fusion = f32[4,256,64,128]{1,3,2,0:T(8,128)} fusion(f32[4,256,32,128]{1,3,2,0:T(8,128)} %get-tuple-element.14, f32[4,256,32,128]{1,3,2,0:T(8,128)S(1)} %get-tuple-element.13), kind=kLoop, calls=%fused_computation | loop fusion | flops 8388608 | bytes 67108864 | tf_op jit(solution)/shard_map/concatenate | solution.py:42
  158.5 31.8 %copy.178 = f32[4,256,64,128]{3,2,1,0:T(8,128)} copy(f32[4,256,64,128]{1,3,2,0:T(8,128)} %pad_maximum_fusion) | data formatting | bytes 67108864 | tf_op jit(solution)/shard_map/concatenate | solution.py:42
  190.3 24.1 %convolution_bitcast_fusion = f32[4,256,32,128]{3,2,1,0:T(8,128)S(1)} fusion(f32[4,256,64,128]{3,2,1,0:T(8,128)} %copy.178, f32[32,16]{0,1:T(8,128)S(1)} %get-tuple-element.40, f32[32,16]{0,1:T(8,128)S(1)} %get-tuple-element.39, f32[32,16]{0,1:T(8,128)S(1)} %fusion.98), kind=kOutput, calls=%fused_computation.36 | convolution fusion | flops 3221231616 | bytes 50337792 | tf_op jit(solution)/shard_map/...pk,pj->...jk/dot_general | solution.py:21
  244.7 175.5 %all-to-all-done.1 = f32[4,256,2048]{1,0,2:T(4,128)} async-done(((f32[4,256,2048]{1,0,2:T(4,128)}), f32[4,256,2048]{1,0,2:T(4,128)}, u32[]{:S(2)}, u32[]{:S(2)}) %all-to-all-start.1) | async-done | bytes 8388640 | tf_op jit(solution)/shard_map/all_to_all | solution.py:81
  447.6 18.5 %all_to_all.165 = f32[4,2048,256]{1,0,2:T(4,128)} all-to-all(f32[4,2048,256]{1,0,2:T(4,128)} %copy.182), channel_id=1, replica_groups=mesh['tiles'=2,'row'=8,'col'=2] {'col'}, dimensions={2} | all-to-all | bytes 16777216 | tf_op jit(solution)/shard_map/all_to_all | solution.py:80
  471.2 23.0 %fusion.110 = (bf16[1,4,1,128,4096]{4,3,2,1,0:T(8,128)(2,1)}, bf16[1,4,1,128,4096]{4,3,2,1,0:T(8,128)(2,1)}, bf16[1,4,1,128,4096]{4,3,2,1,0:T(8,128)(2,1)}, bf16...) fusion(bf16[2,4,4,128,4096]{4,3,2,1,0:T(8,128)(2,1)} %param.3), kind=kLoop, calls=%fused_computation.172 | loop fusion | bytes 67108864 | tf_op jit(solution)/shard_map/slice | solution.py:102
  571.8 19.7 %fusion.43 = f32[4,128,32,256]{3,1,2,0:T(8,128)} fusion(f32[4,128,128,32]{1,3,2,0:T(8,128)S(1)} %bitcast.133, f32[128,128]{0,1:T(8,128)S(1)} %copy-done.1, f32[128,128]{0,1:T(8,128)S(1)} %copy-done.3), kind=kOutput, calls=%fused_computation.67 | convolution fusion | flops 6442483712 | bytes 25296896 | tf_op jit(solution)/shard_map/...qp,qk->...pk/dot_general | solution.py:17
  591.5 63.4 %all-to-all-done.3 = f32[4,256,2048]{1,0,2:T(4,128)} async-done(((f32[4,256,2048]{1,0,2:T(4,128)}), f32[4,256,2048]{1,0,2:T(4,128)}, u32[]{:S(2)}, u32[]{:S(2)}) %all-to-all-start.3) | async-done | bytes 8388640 | tf_op jit(solution)/shard_map/all_to_all | solution.py:88
  715.7 19.5 %fusion.41 = f32[4,128,32,256]{3,1,2,0:T(8,128)} fusion(f32[4,128,128,32]{1,3,2,0:T(8,128)S(1)} %bitcast.132, f32[128,128]{0,1:T(8,128)S(1)} %copy-done.1, f32[128,128]{0,1:T(8,128)S(1)} %copy-done.3), kind=kOutput, calls=%fused_computation.65 | convolution fusion | flops 6442483712 | bytes 25296896 | tf_op jit(solution)/shard_map/...qp,qk->...pk/dot_general | solution.py:17
  735.2 19.1 %multiply_subtract_fusion.3 = (f32[4,128,32,128]{3,1,2,0:T(8,128)}, f32[4,128,32,128]{3,1,2,0:T(8,128)}) fusion(f32[32,128]{1,0:T(8,128)S(1)} %copy-done.11, f32[32,128]{1,0:T(8,128)S(1)} %copy-done.13, f32[4,128,32,256]{3,1,2,0:T(8,128)} %fusion.41, f32[4,128,32,256]{3,1,2,0:T(8,128)} %fusion.43), kind=kLoop, calls=%fused_computation.72 | loop fusion | flops 16777216 | bytes 50364416 | tf_op jit(solution)/shard_map/sub | solution.py:40
  766.2 33.5 %fusion.11 = f32[4,128,64,128]{3,2,1,0:T(8,128)} fusion(f32[4,128,64,128]{3,1,2,0:T(8,128)} %pad_maximum_fusion.2, f32[32,32]{0,1:T(8,128)S(1)} %get-tuple-element.42, f32[32,32]{0,1:T(8,128)S(1)} %get-tuple-element.41, f32[32,32]{0,1:T(8,128)S(1)} %fusion.95), kind=kOutput, calls=%fused_computation.37 | convolution fusion | flops 3221237760 | bytes 33566720 | tf_op jit(solution)/shard_map/...pk,pj->...jk/dot_general | solution.py:21
  834.9 17.6 %fusion.22 = (f32[4,128,128,32]{1,3,2,0:T(8,128)S(1)}, f32[4,128,128,32]{1,3,2,0:T(8,128)S(1)}) fusion(bf16[4,128,128,32]{1,3,2,0:T(8,128)(2,1)} %bitcast.169, bf16[4,128,128,32]{1,3,2,0:T(8,128)(2,1)} %bitcast.168, bf16[4,128,128,32]{1,3,2,0:T(8,128)(2,1)} %bitcast.167, bf16[4,128,128,32]{1,3,2,0:T(8,128)(2,1)} %bitcast.166, ...), kind=kLoop, calls=%fused_computation.42 | loop fusion | flops 79691776 | bytes 67108864 | tf_op jit(solution)/shard_map/add | solution.py:111
  852.5 19.4 %fusion.39 = f32[4,128,32,256]{3,1,2,0:T(8,128)} fusion(f32[4,128,128,32]{1,3,2,0:T(8,128)S(1)} %get-tuple-element.7, f32[128,128]{0,1:T(8,128)S(1)} %get-tuple-element.43, f32[128,128]{0,1:T(8,128)S(1)} %get-tuple-element.44), kind=kOutput, calls=%fused_computation.63 | convolution fusion | flops 6442483712 | bytes 25296896 | tf_op jit(solution)/shard_map/...qp,qk->...pk/dot_general | solution.py:17
  872.0 19.5 %fusion.37 = f32[4,128,32,256]{3,1,2,0:T(8,128)} fusion(f32[4,128,128,32]{1,3,2,0:T(8,128)S(1)} %get-tuple-element.8, f32[128,128]{0,1:T(8,128)S(1)} %get-tuple-element.43, f32[128,128]{0,1:T(8,128)S(1)} %get-tuple-element.44), kind=kOutput, calls=%fused_computation.61 | convolution fusion | flops 6442483712 | bytes 25296896 | tf_op jit(solution)/shard_map/...qp,qk->...pk/dot_general | solution.py:17
  891.5 19.1 %multiply_subtract_fusion.2 = (f32[4,128,32,128]{3,1,2,0:T(8,128)}, f32[4,128,32,128]{3,1,2,0:T(8,128)}) fusion(f32[32,128]{1,0:T(8,128)S(1)} %copy-done.8, f32[32,128]{1,0:T(8,128)S(1)} %copy-done.9, f32[4,128,32,256]{3,1,2,0:T(8,128)} %fusion.37, f32[4,128,32,256]{3,1,2,0:T(8,128)} %fusion.39), kind=kLoop, calls=%fused_computation.70 | loop fusion | flops 16777216 | bytes 50364416 | tf_op jit(solution)/shard_map/sub | solution.py:40
  922.5 33.5 %fusion.14 = f32[4,128,64,128]{3,2,1,0:T(8,128)} fusion(f32[4,128,64,128]{3,1,2,0:T(8,128)} %pad_maximum_fusion.3, f32[32,32]{0,1:T(8,128)S(1)} %copy-done.6, f32[32,32]{0,1:T(8,128)S(1)} %copy-done.14, f32[32,32]{0,1:T(8,128)S(1)} %copy-done.4), kind=kOutput, calls=%fused_computation.38 | convolution fusion | flops 3221237760 | bytes 33566720 | tf_op jit(solution)/shard_map/...pk,pj->...jk/dot_general | solution.py:21
  987.9 175.7 %all-to-all-done.5 = f32[4,128,4096]{1,0,2:T(4,128)} async-done(((f32[4,128,4096]{1,0,2:T(4,128)}), f32[4,128,4096]{1,0,2:T(4,128)}, u32[]{:S(2)}, u32[]{:S(2)}) %all-to-all-start.5) | async-done | bytes 8388640 | tf_op jit(solution)/shard_map/all_to_all | solution.py:117
  1189.9 18.5 %all_to_all.167 = f32[4,1024,512]{1,0,2:T(4,128)} all-to-all(f32[4,1024,512]{1,0,2:T(4,128)} %copy.221), channel_id=1, replica_groups=mesh['tiles'=2,'row'=8,'col'=2] {'col'}, dimensions={2} | all-to-all | bytes 16777216 | tf_op jit(solution)/shard_map/all_to_all | solution.py:116
  1241.4 155.6 %all-to-all-done.7 = f32[4,128,4096]{1,0,2:T(4,128)} async-done(((f32[4,128,4096]{1,0,2:T(4,128)}), f32[4,128,4096]{1,0,2:T(4,128)}, u32[]{:S(2)}, u32[]{:S(2)}) %all-to-all-start.7) | async-done | bytes 8388640 | tf_op jit(solution)/shard_map/all_to_all | solution.py:124
  1456.7 31.3 %fusion.33 = f32[4,256,32,256]{3,1,2,0:T(8,128)} fusion(f32[4,256,64,32]{1,3,2,0:T(8,128)S(1)} %bitcast.141, f32[64,128]{1,0:T(8,128)S(1)} %get-tuple-element.49, f32[64,128]{1,0:T(8,128)S(1)} %get-tuple-element.50), kind=kOutput, calls=%fused_computation.57 | convolution fusion | flops 6442467328 | bytes 42008576 | tf_op jit(solution)/shard_map/...qp,qk->...pk/dot_general | solution.py:17
  1488.1 31.5 %fusion.35 = f32[4,256,32,256]{3,1,2,0:T(8,128)} fusion(f32[4,256,64,32]{1,3,2,0:T(8,128)S(1)} %bitcast.140, f32[64,128]{1,0:T(8,128)S(1)} %get-tuple-element.49, f32[64,128]{1,0:T(8,128)S(1)} %get-tuple-element.50), kind=kOutput, calls=%fused_computation.59 | convolution fusion | flops 6442467328 | bytes 42008576 | tf_op jit(solution)/shard_map/...qp,qk->...pk/dot_general | solution.py:17
  1519.6 34.7 %multiply_subtract_fusion = (f32[4,256,32,128]{3,1,2,0:T(8,128)}, f32[4,256,32,128]{3,1,2,0:T(8,128)}) fusion(f32[32,128]{1,0:T(8,128)S(1)} %copy-done.8, f32[32,128]{1,0:T(8,128)S(1)} %copy-done.9, f32[4,256,32,256]{3,1,2,0:T(8,128)} %fusion.33, f32[4,256,32,256]{3,1,2,0:T(8,128)} %fusion.35), kind=kLoop, calls=%fused_computation.16 | loop fusion | flops 33554432 | bytes 100696064 | tf_op jit(solution)/shard_map/sub | solution.py:40
  1554.3 23.3 %pad_maximum_fusion.1 = f32[4,256,64,128]{3,1,2,0:T(8,128)} fusion(f32[4,256,32,128]{3,1,2,0:T(8,128)} %get-tuple-element.6, f32[4,256,32,128]{3,1,2,0:T(8,128)} %get-tuple-element.5), kind=kLoop, calls=%fused_computation.1 | loop fusion | flops 8388608 | bytes 67108864 | tf_op jit(solution)/shard_map/concatenate | solution.py:42
  1577.6 47.1 %multiply_bitcast_fusion = f32[4,256,32,128]{3,2,1,0:T(8,128)} fusion(f32[4,256,64,128]{3,1,2,0:T(8,128)} %pad_maximum_fusion.1, f32[32,32]{0,1:T(8,128)S(1)} %copy-done.5, f32[32,32]{0,1:T(8,128)S(1)} %copy-done.7), kind=kOutput, calls=%fused_computation.14 | convolution fusion | flops 3225421824 | bytes 50339840 | tf_op jit(solution)/shard_map/...pk,pj->...jk/dot_general | solution.py:21
  1624.7 15.5 copy.255
  1640.2 31.6 %all_to_all.169 = f32[4,256,4096]{1,0,2:T(4,128)} all-to-all(f32[4,256,4096]{1,0,2:T(4,128)} %bitcast.136), channel_id=1, replica_groups=mesh['tiles'=2,'row'=8,'col'=2] {'col'}, dimensions={2} | all-to-all | bytes 33554432 | tf_op jit(solution)/shard_map/all_to_all | solution.py:135
  1671.8 19.2 %copy.236 = f32[4,2,256,2048]{3,2,1,0:T(8,128)} copy(f32[4,2,256,2048]{2,0,3,1:T(4,128)} %bitcast.137) | data formatting | bytes 33554432 | tf_op jit(solution)/shard_map/all_to_all | solution.py:135
  (103 shorter events, 434.2 us)
Async XLA Ops:
  20.9 23.2 %all-to-all-start = ((f32[4,512,2048]{2,0,1:T(4,128)}), f32[4,512,2048]{2,0,1:T(4,128)}, u32[]{:S(2)}, u32[]{:S(2)}) async-start(f32[4,512,2048]{2,0,1:T(4,128)} %copy.174), calls=%async_computation | async-start | bytes 33554432 | tf_op jit(solution)/shard_map/all_to_all | solution.py:71
  30.9 91.5 %copy-start.10 = (f32[32,128]{1,0:T(8,128)}, f32[32,128]{1,0:T(8,128)S(1)}, u32[]{:S(2)}) copy-start(f32[32,128]{1,0:T(8,128)S(1)} %get-tuple-element.37) | copy-start | bytes 49156
  30.9 91.5 %copy-start.12 = (f32[32,128]{1,0:T(8,128)}, f32[32,128]{1,0:T(8,128)S(1)}, u32[]{:S(2)}) copy-start(f32[32,128]{1,0:T(8,128)S(1)} %get-tuple-element.38) | copy-start | bytes 49156
  31.2 47.1 %copy-start = (f32[128,128]{0,1:T(8,128)}, f32[128,128]{0,1:T(8,128)S(1)}, u32[]{:S(2)}) copy-start(f32[128,128]{0,1:T(8,128)S(1)} %get-tuple-element.35) | copy-start | bytes 196612
  31.2 47.1 %copy-start.2 = (f32[128,128]{0,1:T(8,128)}, f32[128,128]{0,1:T(8,128)S(1)}, u32[]{:S(2)}) copy-start(f32[128,128]{0,1:T(8,128)S(1)} %get-tuple-element.36) | copy-start | bytes 196612
  229.5 190.7 %all-to-all-start.1 = ((f32[4,256,2048]{1,0,2:T(4,128)}), f32[4,256,2048]{1,0,2:T(4,128)}, u32[]{:S(2)}, u32[]{:S(2)}) async-start(f32[4,256,2048]{1,0,2:T(4,128)} %bitcast.144), calls=%async_computation.1 | async-start | bytes 16777216 | tf_op jit(solution)/shard_map/all_to_all | solution.py:81
  466.1 188.8 %all-to-all-start.3 = ((f32[4,256,2048]{1,0,2:T(4,128)}), f32[4,256,2048]{1,0,2:T(4,128)}, u32[]{:S(2)}, u32[]{:S(2)}) async-start(f32[4,256,2048]{1,0,2:T(4,128)} %bitcast.142), calls=%async_computation.3 | async-start | bytes 16777216 | tf_op jit(solution)/shard_map/all_to_all | solution.py:88
  567.8 4.0 copy-start.1
  567.8 4.0 copy-start.3
  715.7 19.6 %copy-start.11 = (f32[32,128]{1,0:T(8,128)S(1)}, f32[32,128]{1,0:T(8,128)}, u32[]{:S(2)}) copy-start(f32[32,128]{1,0:T(8,128)} %copy-done.10) | copy-start | bytes 49156
  715.7 19.6 %copy-start.13 = (f32[32,128]{1,0:T(8,128)S(1)}, f32[32,128]{1,0:T(8,128)}, u32[]{:S(2)}) copy-start(f32[32,128]{1,0:T(8,128)} %copy-done.12) | copy-start | bytes 49156
  871.9 19.5 %copy-start.8 = (f32[32,128]{1,0:T(8,128)S(1)}, f32[32,128]{1,0:T(8,128)}, u32[]{:S(2)}) copy-start(f32[32,128]{1,0:T(8,128)} %get-tuple-element.45) | copy-start | bytes 49156
  872.0 19.5 %copy-start.9 = (f32[32,128]{1,0:T(8,128)S(1)}, f32[32,128]{1,0:T(8,128)}, u32[]{:S(2)}) copy-start(f32[32,128]{1,0:T(8,128)} %get-tuple-element.46) | copy-start | bytes 49156
  910.6 11.9 copy-start.4
  910.6 11.9 copy-start.6
  910.6 11.9 copy-start.14
  975.0 188.6 %all-to-all-start.5 = ((f32[4,128,4096]{1,0,2:T(4,128)}), f32[4,128,4096]{1,0,2:T(4,128)}, u32[]{:S(2)}, u32[]{:S(2)}) async-start(f32[4,128,4096]{1,0,2:T(4,128)} %bitcast.145), calls=%async_computation.5 | async-start | bytes 16777216 | tf_op jit(solution)/shard_map/all_to_all | solution.py:117
  1208.4 188.6 %all-to-all-start.7 = ((f32[4,128,4096]{1,0,2:T(4,128)}), f32[4,128,4096]{1,0,2:T(4,128)}, u32[]{:S(2)}, u32[]{:S(2)}) async-start(f32[4,128,4096]{1,0,2:T(4,128)} %bitcast.143), calls=%async_computation.7 | async-start | bytes 16777216 | tf_op jit(solution)/shard_map/all_to_all | solution.py:124
  1452.6 35.5 %slice-start = ((s8[8388608]{0:T(1024)(128)(4,1)}), s8[4194304]{0:T(1024)(128)(4,1)S(1)}, s32[]{:S(2)}) async-start(s8[8388608]{0:T(1024)(128)(4,1)} %bitcast.138), calls=%async_computation.10 | async-start | bytes 8388608
  1456.7 31.3 %slice-start.1 = ((s8[8388608]{0:T(1024)(128)(4,1)}), s8[4194304]{0:T(1024)(128)(4,1)S(1)}, s32[]{:S(2)}) async-start(s8[8388608]{0:T(1024)(128)(4,1)} %bitcast.138), calls=%async_computation.11 | async-start | bytes 8388608
  1554.3 23.3 %copy-start.5 = (f32[32,32]{0,1:T(8,128)S(1)}, f32[32,32]{0,1:T(8,128)}, u32[]{:S(2)}) copy-start(f32[32,32]{0,1:T(8,128)} %fusion.94) | copy-start | bytes 12292
  1554.3 23.3 %copy-start.7 = (f32[32,32]{0,1:T(8,128)S(1)}, f32[32,32]{0,1:T(8,128)}, u32[]{:S(2)}) copy-start(f32[32,32]{0,1:T(8,128)} %get-tuple-element.48) | copy-start | bytes 12292
where the time goes:
time: 1700 us; the launch traced here: 1690 us
  waiting for transfers between devices  583 us (34%)
  local copies, waits for them, and re-layouts  482 us (28%)
  matrix products  323 us (19%)
  other arithmetic  177 us (10%)
  blocking collectives  93.3 us (5%)
  starting transfers between devices  32.1 us (2%)
    dot_general x7, matrix products, contract_first(): jnp.einsum('...qp,qk->...pk', values, table, precision=lax.Precision.HIGH...  185 us
    all_to_all x1, waiting for transfers between devices, shards(): lax.all_to_all(back_real, 'row', split_axis=2, concat_axis=1, tiled=True)  176 us
    all_to_all x1, waiting for transfers between devices, shards(): lax.all_to_all(spec_real, 'row', split_axis=2, concat_axis=1, tiled=True)  175 us
    all_to_all x1, waiting for transfers between devices, shards(): lax.all_to_all(back_imag, 'row', split_axis=2, concat_axis=1, tiled=True)  156 us
    dot_general x4, matrix products, contract_second(): jnp.einsum('...pk,pj->...jk', values, table, precision=lax.Precision.HIGH...  138 us
    sub x4, other arithmetic, fourier(): turned_real = part_real * twist_cos - part_imag * twist_sin  90.5 us
    unnamed x43, local copies, waits for them, and re-layouts  71.9 us
    concatenate x4, other arithmetic, fourier(): stacked = jnp.concatenate([turned_real, turned_imag], axis=-2)  65.5 us
  transfers between devices with their start and end apart: 5, of which 5 were waited for; matrix products, arithmetic and copies ran while one was open for 10% of the time, Pallas kernels for 0%

commit v1 on v0

--- a/solution.py
+++ b/solution.py
@@ -3,6 +3,22 @@
 import jax.numpy as jnp
 from jax import lax
 from jax.sharding import PartitionSpec as P
+
+
+def swapped_with_each(array, axis, split, join):
+    ways, here = (lax.axis_size(axis), lax.axis_index(axis))
+    width = array.shape[split] // ways
+    dims = list(array.shape)
+    dims[split] = width
+    height = dims[join]
+    dims[join] = height * ways
+    full = jnp.zeros(dims, array.dtype)
+    for mask in range(ways):
+        part = lax.dynamic_slice_in_dim(array, (here ^ mask) * width, width, axis=split)
+        if mask:
+            part = lax.ppermute(part, axis, [(d, d ^ mask) for d in range(ways)])
+        full = lax.dynamic_update_slice_in_dim(full, part, (here ^ mask) * height, axis=join)
+    return full
 
 
 def phase_pair(first_len, second_len, period, sign):
@@ -78,7 +94,7 @@
     )
     moved_real, moved_imag = (
         lax.all_to_all(
-            lax.all_to_all(spec_real, "row", split_axis=2, concat_axis=1, tiled=True),
+            swapped_with_each(spec_real, "row", 2, 1),
             "col",
             split_axis=2,
             concat_axis=1,

time: 1700 us -> 1690 us (level)
  waiting for transfers between devices: 583 us -> 522 us
  starting transfers between devices: 32.1 us -> 76.4 us
    all_to_all x1 -> x0, waiting for transfers between devices: 175 us -> none  [shards(): lax.all_to_all(spec_real, 'row', split_axis=2, concat_axis=1, tiled=True)]
    ppermute x0 -> x7, waiting for transfers between devices: none -> 113 us  [swapped_with_each(): part = lax.ppermute(part, axis, [(d, d ^ mask) for d in range(ways)])]
    all_to_all x1, starting transfers between devices: 5.14 us -> 42.7 us  [shards(): lax.all_to_all(spec_imag, 'row', split_axis=2, concat_axis=1, tiled=True)]
    all_to_all x5 -> x2, local copies, waits for them, and re-layouts: 47.6 us -> 20.2 us  [shards(): lax.all_to_all(swapped_with_each(spec_real, 'row', 2, 1), 'col', split_ax...]
    dynamic_update_slice x0 -> x7, local copies, waits for them, and re-layouts: none -> 17.1 us  [swapped_with_each(): lax.dynamic_update_slice_in_dim(full, part, (here ^ mask) * height, axis=...]
    unnamed x43 -> x51, local copies, waits for them, and re-layouts: 71.9 us -> 76.2 us
  transfers between devices with their start and end apart: 5 -> 11, of which waited for: 5 -> 7; matrix products, arithmetic and copies ran while one was open for 10% -> 11% of each run, Pallas kernels for 0% -> 0%
where the time goes in v1:
time: 1690 us; the launch traced here: 1670 us
  waiting for transfers between devices  522 us (31%)
  local copies, waits for them, and re-layouts  481 us (28%)
  matrix products  323 us (19%)
  other arithmetic  177 us (10%)
  blocking collectives  93.4 us (6%)
  starting transfers between devices  76.4 us (5%)
    dot_general x7, matrix products, contract_first(): jnp.einsum('...qp,qk->...pk', values, table, precision=lax.Precision.HIGH...  185 us
    all_to_all x1, waiting for transfers between devices, shards(): lax.all_to_all(back_real, 'row', split_axis=2, concat_axis=1, tiled=True)  176 us
    all_to_all x1, waiting for transfers between devices, shards(): lax.all_to_all(back_imag, 'row', split_axis=2, concat_axis=1, tiled=True)  156 us
    dot_general x4, matrix products, contract_second(): jnp.einsum('...pk,pj->...jk', values, table, precision=lax.Precision.HIGH...  138 us
    ppermute x7, waiting for transfers between devices, swapped_with_each(): part = lax.ppermute(part, axis, [(d, d ^ mask) for d in range(ways)])  113 us
    sub x4, other arithmetic, fourier(): turned_real = part_real * twist_cos - part_imag * twist_sin  90.5 us
    unnamed x51, local copies, waits for them, and re-layouts  76.2 us
    concatenate x4, other arithmetic, fourier(): stacked = jnp.concatenate([turned_real, turned_imag], axis=-2)  65.5 us
  transfers between devices with their start and end apart: 11, of which 7 were waited for; matrix products, arithmetic and copies ran while one was open for 11% of the time, Pallas kernels for 0%

profile of v1, /device:TPU:0, one launch (start us, length us, event | category | flops | bytes accessed | tf_op | source)
XLA Modules:
  0.0 1674.8 jit_solution(10376778094193105740)
XLA Ops:
  0.0 20.9 %copy.232 = f32[4,512,2048]{2,0,1:T(4,128)} copy(f32[4,512,2048]{2,1,0:T(8,128)} %param.2) | data formatting | bytes 33554432 | tf_op args[0]
  44.2 17.8 %copy.233 = f32[4,512,2048]{2,1,0:T(8,128)} copy(f32[4,512,2048]{2,0,1:T(4,128)} %all-to-all-done) | data formatting | bytes 33554432 | tf_op jit(solution)/shard_map/all_to_all | solution.py:87
  78.3 44.1 %fusion.8 = f32[4,256,32,256]{1,3,2,0:T(8,128)} fusion(f32[4,256,128,32]{1,3,2,0:T(8,128)} %bitcast.130, f32[128,128]{0,1:T(8,128)S(1)} %get-tuple-element.43, f32[128,128]{0,1:T(8,128)S(1)} %get-tuple-element.44), kind=kOutput, calls=%fused_computation.19 | convolution fusion | flops 12884934656 | bytes 50462720 | tf_op jit(solution)/shard_map/...qp,qk->...pk/dot_general | solution.py:33
  122.4 17.6 %multiply_subtract_fusion.1 = (f32[4,256,32,128]{1,3,2,0:T(8,128)S(1)}, f32[4,256,32,128]{1,3,2,0:T(8,128)}) fusion(f32[4,256,32,256]{1,3,2,0:T(8,128)} %fusion.8, f32[32,128]{1,0:T(8,128)S(1)} %get-tuple-element.45, f32[32,128]{1,0:T(8,128)S(1)} %get-tuple-element.46), kind=kLoop, calls=%fused_computation.18 | loop fusion | flops 25165824 | bytes 67141632 | tf_op jit(solution)/shard_map/sub | solution.py:56
  140.0 18.5 %pad_maximum_fusion = f32[4,256,64,128]{1,3,2,0:T(8,128)} fusion(f32[4,256,32,128]{1,3,2,0:T(8,128)} %get-tuple-element.14, f32[4,256,32,128]{1,3,2,0:T(8,128)S(1)} %get-tuple-element.13), kind=kLoop, calls=%fused_computation | loop fusion | flops 8388608 | bytes 67108864 | tf_op jit(solution)/shard_map/concatenate | solution.py:58
  158.5 31.8 %copy.236 = f32[4,256,64,128]{3,2,1,0:T(8,128)} copy(f32[4,256,64,128]{1,3,2,0:T(8,128)} %pad_maximum_fusion) | data formatting | bytes 67108864 | tf_op jit(solution)/shard_map/concatenate | solution.py:58
  190.3 24.1 %convolution_bitcast_fusion = f32[4,256,32,128]{3,2,1,0:T(8,128)S(1)} fusion(f32[4,256,64,128]{3,2,1,0:T(8,128)} %copy.236, f32[32,16]{0,1:T(8,128)S(1)} %get-tuple-element.48, f32[32,16]{0,1:T(8,128)S(1)} %get-tuple-element.47, f32[32,16]{0,1:T(8,128)S(1)} %fusion.98), kind=kOutput, calls=%fused_computation.36 | convolution fusion | flops 3221231616 | bytes 50337792 | tf_op jit(solution)/shard_map/...pk,pj->...jk/dot_general | solution.py:37
  248.0 62.0 %collective-permute-done.1 = f32[4,256,256]{1,0,2:T(4,128)S(1)} collective-permute-done((f32[4,256,256]{1,0,2:T(4,128)}, f32[4,256,256]{1,0,2:T(4,128)S(1)}, u32[]{:S(2)}, u32[]{:S(2)}) %collective-permute-start.1) | collective-permute-done | bytes 1048608 | tf_op jit(solution)/shard_map/ppermute | solution.py:19
  338.0 46.4 %collective-permute-done.4 = f32[4,256,256]{1,0,2:T(4,128)} collective-permute-done((f32[4,256,256]{1,0,2:T(4,128)S(1)}, f32[4,256,256]{1,0,2:T(4,128)}, u32[]{:S(2)}, u32[]{:S(2)}) %collective-permute-start.4) | collective-permute-done | bytes 1048608 | tf_op jit(solution)/shard_map/ppermute | solution.py:19
  391.7 18.6 %all_to_all.147 = f32[4,2048,256]{1,0,2:T(4,128)} all-to-all(f32[4,2048,256]{1,0,2:T(4,128)} %constant_dynamic-update-slice_fusion), channel_id=1, replica_groups=mesh['tiles'=2,'row'=8,'col'=2] {'col'}, dimensions={2} | all-to-all | bytes 16777216 | tf_op jit(solution)/shard_map/all_to_all | solution.py:96
  410.3 42.7 %all-to-all-start.2 = ((f32[4,256,2048]{1,0,2:T(4,128)}), f32[4,256,2048]{1,0,2:T(4,128)}, u32[]{:S(2)}, u32[]{:S(2)}) async-start(f32[4,256,2048]{1,0,2:T(4,128)} %bitcast.139), calls=%async_computation.2 | async-start | bytes 16777216 | tf_op jit(solution)/shard_map/all_to_all | solution.py:104
  453.1 23.0 %fusion.110 = (bf16[1,4,1,128,4096]{4,3,2,1,0:T(8,128)(2,1)}, bf16[1,4,1,128,4096]{4,3,2,1,0:T(8,128)(2,1)}, bf16[1,4,1,128,4096]{4,3,2,1,0:T(8,128)(2,1)}, bf16...) fusion(bf16[2,4,4,128,4096]{4,3,2,1,0:T(8,128)(2,1)} %param.3), kind=kLoop, calls=%fused_computation.187 | loop fusion | bytes 67108864 | tf_op jit(solution)/shard_map/slice | solution.py:118
  553.5 19.7 %fusion.43 = f32[4,128,32,256]{3,1,2,0:T(8,128)} fusion(f32[4,128,128,32]{1,3,2,0:T(8,128)S(1)} %bitcast.129, f32[128,128]{0,1:T(8,128)S(1)} %copy-done.3, f32[128,128]{0,1:T(8,128)S(1)} %copy-done.5), kind=kOutput, calls=%fused_computation.67 | convolution fusion | flops 6442483712 | bytes 25296896 | tf_op jit(solution)/shard_map/...qp,qk->...pk/dot_general | solution.py:33
  573.2 64.8 %all-to-all-done.2 = f32[4,256,2048]{1,0,2:T(4,128)} async-done(((f32[4,256,2048]{1,0,2:T(4,128)}), f32[4,256,2048]{1,0,2:T(4,128)}, u32[]{:S(2)}, u32[]{:S(2)}) %all-to-all-start.2) | async-done | bytes 8388640 | tf_op jit(solution)/shard_map/all_to_all | solution.py:104
  698.9 19.5 %fusion.41 = f32[4,128,32,256]{3,1,2,0:T(8,128)} fusion(f32[4,128,128,32]{1,3,2,0:T(8,128)S(1)} %bitcast.128, f32[128,128]{0,1:T(8,128)S(1)} %copy-done.3, f32[128,128]{0,1:T(8,128)S(1)} %copy-done.5), kind=kOutput, calls=%fused_computation.65 | convolution fusion | flops 6442483712 | bytes 25296896 | tf_op jit(solution)/shard_map/...qp,qk->...pk/dot_general | solution.py:33
  718.4 19.1 %multiply_subtract_fusion.3 = (f32[4,128,32,128]{3,1,2,0:T(8,128)}, f32[4,128,32,128]{3,1,2,0:T(8,128)}) fusion(f32[32,128]{1,0:T(8,128)S(1)} %copy-done.15, f32[32,128]{1,0:T(8,128)S(1)} %copy-done.17, f32[4,128,32,256]{3,1,2,0:T(8,128)} %fusion.41, f32[4,128,32,256]{3,1,2,0:T(8,128)} %fusion.43), kind=kLoop, calls=%fused_computation.72 | loop fusion | flops 16777216 | bytes 50364416 | tf_op jit(solution)/shard_map/sub | solution.py:56
  749.4 33.5 %fusion.11 = f32[4,128,64,128]{3,2,1,0:T(8,128)} fusion(f32[4,128,64,128]{3,1,2,0:T(8,128)} %pad_maximum_fusion.2, f32[32,32]{0,1:T(8,128)S(1)} %get-tuple-element.50, f32[32,32]{0,1:T(8,128)S(1)} %get-tuple-element.49, f32[32,32]{0,1:T(8,128)S(1)} %fusion.95), kind=kOutput, calls=%fused_computation.37 | convolution fusion | flops 3221237760 | bytes 33566720 | tf_op jit(solution)/shard_map/...pk,pj->...jk/dot_general | solution.py:37
  818.1 17.6 %fusion.22 = (f32[4,128,128,32]{1,3,2,0:T(8,128)S(1)}, f32[4,128,128,32]{1,3,2,0:T(8,128)S(1)}) fusion(bf16[4,128,128,32]{1,3,2,0:T(8,128)(2,1)} %bitcast.163, bf16[4,128,128,32]{1,3,2,0:T(8,128)(2,1)} %bitcast.162, bf16[4,128,128,32]{1,3,2,0:T(8,128)(2,1)} %bitcast.161, bf16[4,128,128,32]{1,3,2,0:T(8,128)(2,1)} %bitcast.160, ...), kind=kLoop, calls=%fused_computation.42 | loop fusion | flops 79691776 | bytes 67108864 | tf_op jit(solution)/shard_map/add | solution.py:127
  835.7 19.4 %fusion.39 = f32[4,128,32,256]{3,1,2,0:T(8,128)} fusion(f32[4,128,128,32]{1,3,2,0:T(8,128)S(1)} %get-tuple-element.7, f32[128,128]{0,1:T(8,128)S(1)} %get-tuple-element.51, f32[128,128]{0,1:T(8,128)S(1)} %get-tuple-element.52), kind=kOutput, calls=%fused_computation.63 | convolution fusion | flops 6442483712 | bytes 25296896 | tf_op jit(solution)/shard_map/...qp,qk->...pk/dot_general | solution.py:33
  855.2 19.5 %fusion.37 = f32[4,128,32,256]{3,1,2,0:T(8,128)} fusion(f32[4,128,128,32]{1,3,2,0:T(8,128)S(1)} %get-tuple-element.8, f32[128,128]{0,1:T(8,128)S(1)} %get-tuple-element.51, f32[128,128]{0,1:T(8,128)S(1)} %get-tuple-element.52), kind=kOutput, calls=%fused_computation.61 | convolution fusion | flops 6442483712 | bytes 25296896 | tf_op jit(solution)/shard_map/...qp,qk->...pk/dot_general | solution.py:33
  874.7 19.1 %multiply_subtract_fusion.2 = (f32[4,128,32,128]{3,1,2,0:T(8,128)}, f32[4,128,32,128]{3,1,2,0:T(8,128)}) fusion(f32[32,128]{1,0:T(8,128)S(1)} %copy-done.12, f32[32,128]{1,0:T(8,128)S(1)} %copy-done.13, f32[4,128,32,256]{3,1,2,0:T(8,128)} %fusion.37, f32[4,128,32,256]{3,1,2,0:T(8,128)} %fusion.39), kind=kLoop, calls=%fused_computation.70 | loop fusion | flops 16777216 | bytes 50364416 | tf_op jit(solution)/shard_map/sub | solution.py:56
  905.7 33.5 %fusion.14 = f32[4,128,64,128]{3,2,1,0:T(8,128)} fusion(f32[4,128,64,128]{3,1,2,0:T(8,128)} %pad_maximum_fusion.3, f32[32,32]{0,1:T(8,128)S(1)} %copy-done.10, f32[32,32]{0,1:T(8,128)S(1)} %copy-done.18, f32[32,32]{0,1:T(8,128)S(1)} %copy-done.8), kind=kOutput, calls=%fused_computation.38 | convolution fusion | flops 3221237760 | bytes 33566720 | tf_op jit(solution)/shard_map/...pk,pj->...jk/dot_general | solution.py:37
  971.2 175.7 %all-to-all-done.4 = f32[4,128,4096]{1,0,2:T(4,128)} async-done(((f32[4,128,4096]{1,0,2:T(4,128)}), f32[4,128,4096]{1,0,2:T(4,128)}, u32[]{:S(2)}, u32[]{:S(2)}) %all-to-all-start.4) | async-done | bytes 8388640 | tf_op jit(solution)/shard_map/all_to_all | solution.py:133
  1173.3 18.5 %all_to_all.149 = f32[4,1024,512]{1,0,2:T(4,128)} all-to-all(f32[4,1024,512]{1,0,2:T(4,128)} %copy.283), channel_id=1, replica_groups=mesh['tiles'=2,'row'=8,'col'=2] {'col'}, dimensions={2} | all-to-all | bytes 16777216 | tf_op jit(solution)/shard_map/all_to_all | solution.py:132
  1224.7 155.6 %all-to-all-done.6 = f32[4,128,4096]{1,0,2:T(4,128)} async-done(((f32[4,128,4096]{1,0,2:T(4,128)}), f32[4,128,4096]{1,0,2:T(4,128)}, u32[]{:S(2)}, u32[]{:S(2)}) %all-to-all-start.6) | async-done | bytes 8388640 | tf_op jit(solution)/shard_map/all_to_all | solution.py:140
  1440.1 31.4 %fusion.33 = f32[4,256,32,256]{3,1,2,0:T(8,128)} fusion(f32[4,256,64,32]{1,3,2,0:T(8,128)S(1)} %bitcast.137, f32[64,128]{1,0:T(8,128)S(1)} %get-tuple-element.57, f32[64,128]{1,0:T(8,128)S(1)} %get-tuple-element.58), kind=kOutput, calls=%fused_computation.57 | convolution fusion | flops 6442467328 | bytes 42008576 | tf_op jit(solution)/shard_map/...qp,qk->...pk/dot_general | solution.py:33
  1471.5 31.5 %fusion.35 = f32[4,256,32,256]{3,1,2,0:T(8,128)} fusion(f32[4,256,64,32]{1,3,2,0:T(8,128)S(1)} %bitcast.136, f32[64,128]{1,0:T(8,128)S(1)} %get-tuple-element.57, f32[64,128]{1,0:T(8,128)S(1)} %get-tuple-element.58), kind=kOutput, calls=%fused_computation.59 | convolution fusion | flops 6442467328 | bytes 42008576 | tf_op jit(solution)/shard_map/...qp,qk->...pk/dot_general | solution.py:33
  1503.1 34.7 %multiply_subtract_fusion = (f32[4,256,32,128]{3,1,2,0:T(8,128)}, f32[4,256,32,128]{3,1,2,0:T(8,128)}) fusion(f32[32,128]{1,0:T(8,128)S(1)} %copy-done.12, f32[32,128]{1,0:T(8,128)S(1)} %copy-done.13, f32[4,256,32,256]{3,1,2,0:T(8,128)} %fusion.33, f32[4,256,32,256]{3,1,2,0:T(8,128)} %fusion.35), kind=kLoop, calls=%fused_computation.16 | loop fusion | flops 33554432 | bytes 100696064 | tf_op jit(solution)/shard_map/sub | solution.py:56
  1537.7 23.3 %pad_maximum_fusion.1 = f32[4,256,64,128]{3,1,2,0:T(8,128)} fusion(f32[4,256,32,128]{3,1,2,0:T(8,128)} %get-tuple-element.6, f32[4,256,32,128]{3,1,2,0:T(8,128)} %get-tuple-element.5), kind=kLoop, calls=%fused_computation.1 | loop fusion | flops 8388608 | bytes 67108864 | tf_op jit(solution)/shard_map/concatenate | solution.py:58
  1561.0 47.1 %multiply_bitcast_fusion = f32[4,256,32,128]{3,2,1,0:T(8,128)} fusion(f32[4,256,64,128]{3,1,2,0:T(8,128)} %pad_maximum_fusion.1, f32[32,32]{0,1:T(8,128)S(1)} %copy-done.9, f32[32,32]{0,1:T(8,128)S(1)} %copy-done.11), kind=kOutput, calls=%fused_computation.14 | convolution fusion | flops 3225421824 | bytes 50339840 | tf_op jit(solution)/shard_map/...pk,pj->...jk/dot_general | solution.py:37
  1623.6 31.6 %all_to_all.151 = f32[4,256,4096]{1,0,2:T(4,128)} all-to-all(f32[4,256,4096]{1,0,2:T(4,128)} %bitcast.132), channel_id=1, replica_groups=mesh['tiles'=2,'row'=8,'col'=2] {'col'}, dimensions={2} | all-to-all | bytes 33554432 | tf_op jit(solution)/shard_map/all_to_all | solution.py:151
  1655.2 19.2 %copy.298 = f32[4,2,256,2048]{3,2,1,0:T(8,128)} copy(f32[4,2,256,2048]{2,0,3,1:T(4,128)} %bitcast.133) | data formatting | bytes 33554432 | tf_op jit(solution)/shard_map/all_to_all | solution.py:151
  (129 shorter events, 472.1 us)
Async XLA Ops:
  20.9 23.3 %all-to-all-start = ((f32[4,512,2048]{2,0,1:T(4,128)}), f32[4,512,2048]{2,0,1:T(4,128)}, u32[]{:S(2)}, u32[]{:S(2)}) async-start(f32[4,512,2048]{2,0,1:T(4,128)} %copy.232), calls=%async_computation | async-start | bytes 33554432 | tf_op jit(solution)/shard_map/all_to_all | solution.py:87
  30.9 91.4 %copy-start.14 = (f32[32,128]{1,0:T(8,128)}, f32[32,128]{1,0:T(8,128)S(1)}, u32[]{:S(2)}) copy-start(f32[32,128]{1,0:T(8,128)S(1)} %get-tuple-element.45) | copy-start | bytes 49156
  31.0 91.4 %copy-start.16 = (f32[32,128]{1,0:T(8,128)}, f32[32,128]{1,0:T(8,128)S(1)}, u32[]{:S(2)}) copy-start(f32[32,128]{1,0:T(8,128)S(1)} %get-tuple-element.46) | copy-start | bytes 49156
  31.2 47.1 %copy-start.2 = (f32[128,128]{0,1:T(8,128)}, f32[128,128]{0,1:T(8,128)S(1)}, u32[]{:S(2)}) copy-start(f32[128,128]{0,1:T(8,128)S(1)} %get-tuple-element.43) | copy-start | bytes 196612
  31.3 47.1 %copy-start.4 = (f32[128,128]{0,1:T(8,128)}, f32[128,128]{0,1:T(8,128)S(1)}, u32[]{:S(2)}) copy-start(f32[128,128]{0,1:T(8,128)S(1)} %get-tuple-element.44) | copy-start | bytes 196612
  229.5 3.4 copy-start
  235.9 3.3 copy-start.1
  239.2 70.8 %collective-permute-start.1 = (f32[4,256,256]{1,0,2:T(4,128)}, f32[4,256,256]{1,0,2:T(4,128)S(1)}, u32[]{:S(2)}, u32[]{:S(2)}) collective-permute-start(f32[4,256,256]{1,0,2:T(4,128)} %get-tuple-element.40), channel_id=1, source_target_pairs={{0,4},{2,6},{4,0},{6,2},{8,12},{10,14},{12,8},{14,10},{1,5},{3,7},... | collective-permute-start | bytes 3145736 | tf_op jit(solution)/shard_map/ppermute | solution.py:19
  242.2 69.5 %collective-permute-start = (f32[4,256,256]{1,0,2:T(4,128)}, f32[4,256,256]{1,0,2:T(4,128)S(1)}, u32[]{:S(2)}, u32[]{:S(2)}) collective-permute-start(f32[4,256,256]{1,0,2:T(4,128)} %get-tuple-element.41), channel_id=1, source_target_pairs={{0,2},{2,0},{4,6},{6,4},{8,10},{10,8},{12,14},{14,12},{1,3},{3,1},... | collective-permute-start | bytes 3145736 | tf_op jit(solution)/shard_map/ppermute | solution.py:19
  243.7 89.4 %collective-permute-start.2 = (f32[4,256,256]{1,0,2:T(4,128)}, f32[4,256,256]{1,0,2:T(4,128)}, u32[]{:S(2)}, u32[]{:S(2)}) collective-permute-start(f32[4,256,256]{1,0,2:T(4,128)} %get-tuple-element.39), channel_id=1, source_target_pairs={{0,6},{2,4},{4,2},{6,0},{8,14},{10,12},{12,10},{14,8},{1,7},{3,5},... | collective-permute-start | bytes 3145736 | tf_op jit(solution)/shard_map/ppermute | solution.py:19
  243.7 91.8 %collective-permute-start.3 = (f32[4,256,256]{1,0,2:T(4,128)}, f32[4,256,256]{1,0,2:T(4,128)}, u32[]{:S(2)}, u32[]{:S(2)}) collective-permute-start(f32[4,256,256]{1,0,2:T(4,128)} %get-tuple-element.38), channel_id=1, source_target_pairs={{0,8},{2,10},{4,12},{6,14},{8,0},{10,2},{12,4},{14,6},{1,9},{3,11}... | collective-permute-start | bytes 3145736 | tf_op jit(solution)/shard_map/ppermute | solution.py:19
  246.8 137.7 %collective-permute-start.4 = (f32[4,256,256]{1,0,2:T(4,128)S(1)}, f32[4,256,256]{1,0,2:T(4,128)}, u32[]{:S(2)}, u32[]{:S(2)}) collective-permute-start(f32[4,256,256]{1,0,2:T(4,128)S(1)} %get-tuple-element.37), channel_id=1, source_target_pairs={{0,10},{2,8},{4,14},{6,12},{8,2},{10,0},{12,6},{14,4},{1,11},{3,9}... | collective-permute-start | bytes 3145736 | tf_op jit(solution)/shard_map/ppermute | solution.py:19
  310.0 5.2 copy-start.6
  310.0 76.9 %collective-permute-start.5 = (f32[4,256,256]{1,0,2:T(4,128)S(1)}, f32[4,256,256]{1,0,2:T(4,128)}, u32[]{:S(2)}, u32[]{:S(2)}) collective-permute-start(f32[4,256,256]{1,0,2:T(4,128)S(1)} %get-tuple-element.36), channel_id=1, source_target_pairs={{0,12},{2,14},{4,8},{6,10},{8,4},{10,6},{12,0},{14,2},{1,13},{3,15... | collective-permute-start | bytes 3145736 | tf_op jit(solution)/shard_map/ppermute | solution.py:19
  311.8 3.4 copy-start.7
  311.8 77.5 %collective-permute-start.6 = (f32[4,256,256]{1,0,2:T(4,128)S(1)}, f32[4,256,256]{1,0,2:T(4,128)}, u32[]{:S(2)}, u32[]{:S(2)}) collective-permute-start(f32[4,256,256]{1,0,2:T(4,128)S(1)} %get-tuple-element.35), channel_id=1, source_target_pairs={{0,14},{2,12},{4,10},{6,8},{8,6},{10,4},{12,2},{14,0},{1,15},{3,13... | collective-permute-start | bytes 3145736 | tf_op jit(solution)/shard_map/ppermute | solution.py:19
  410.3 227.6 %all-to-all-start.2 = ((f32[4,256,2048]{1,0,2:T(4,128)}), f32[4,256,2048]{1,0,2:T(4,128)}, u32[]{:S(2)}, u32[]{:S(2)}) async-start(f32[4,256,2048]{1,0,2:T(4,128)} %bitcast.139), calls=%async_computation.2 | async-start | bytes 16777216 | tf_op jit(solution)/shard_map/all_to_all | solution.py:104
  549.5 4.0 copy-start.3
  549.5 4.0 copy-start.5
  698.9 19.6 %copy-start.15 = (f32[32,128]{1,0:T(8,128)S(1)}, f32[32,128]{1,0:T(8,128)}, u32[]{:S(2)}) copy-start(f32[32,128]{1,0:T(8,128)} %copy-done.14) | copy-start | bytes 49156
  698.9 19.6 %copy-start.17 = (f32[32,128]{1,0:T(8,128)S(1)}, f32[32,128]{1,0:T(8,128)}, u32[]{:S(2)}) copy-start(f32[32,128]{1,0:T(8,128)} %copy-done.16) | copy-start | bytes 49156
  855.2 19.5 %copy-start.12 = (f32[32,128]{1,0:T(8,128)S(1)}, f32[32,128]{1,0:T(8,128)}, u32[]{:S(2)}) copy-start(f32[32,128]{1,0:T(8,128)} %get-tuple-element.53) | copy-start | bytes 49156
  855.2 19.5 %copy-start.13 = (f32[32,128]{1,0:T(8,128)S(1)}, f32[32,128]{1,0:T(8,128)}, u32[]{:S(2)}) copy-start(f32[32,128]{1,0:T(8,128)} %get-tuple-element.54) | copy-start | bytes 49156
  893.8 11.9 copy-start.8
  893.8 11.9 copy-start.10
  893.8 11.9 copy-start.18
  958.2 188.6 %all-to-all-start.4 = ((f32[4,128,4096]{1,0,2:T(4,128)}), f32[4,128,4096]{1,0,2:T(4,128)}, u32[]{:S(2)}, u32[]{:S(2)}) async-start(f32[4,128,4096]{1,0,2:T(4,128)} %bitcast.141), calls=%async_computation.4 | async-start | bytes 16777216 | tf_op jit(solution)/shard_map/all_to_all | solution.py:133
  1191.7 188.6 %all-to-all-start.6 = ((f32[4,128,4096]{1,0,2:T(4,128)}), f32[4,128,4096]{1,0,2:T(4,128)}, u32[]{:S(2)}, u32[]{:S(2)}) async-start(f32[4,128,4096]{1,0,2:T(4,128)} %bitcast.140), calls=%async_computation.6 | async-start | bytes 16777216 | tf_op jit(solution)/shard_map/all_to_all | solution.py:140
  1436.0 35.5 %slice-start = ((s8[8388608]{0:T(1024)(128)(4,1)}), s8[4194304]{0:T(1024)(128)(4,1)S(1)}, s32[]{:S(2)}) async-start(s8[8388608]{0:T(1024)(128)(4,1)} %bitcast.134), calls=%async_computation.9 | async-start | bytes 8388608
  1440.1 31.4 %slice-start.1 = ((s8[8388608]{0:T(1024)(128)(4,1)}), s8[4194304]{0:T(1024)(128)(4,1)S(1)}, s32[]{:S(2)}) async-start(s8[8388608]{0:T(1024)(128)(4,1)} %bitcast.134), calls=%async_computation.10 | async-start | bytes 8388608
  1537.7 23.3 %copy-start.9 = (f32[32,32]{0,1:T(8,128)S(1)}, f32[32,32]{0,1:T(8,128)}, u32[]{:S(2)}) copy-start(f32[32,32]{0,1:T(8,128)} %fusion.94) | copy-start | bytes 12292
  1537.7 23.3 %copy-start.11 = (f32[32,32]{0,1:T(8,128)S(1)}, f32[32,32]{0,1:T(8,128)}, u32[]{:S(2)}) copy-start(f32[32,32]{0,1:T(8,128)} %get-tuple-element.56) | copy-start | bytes 12292
